TPU v7x, 32 devices: a whole 2x2x4 slice. The times are simulated.
32 devices in a mesh: cable: 2 (over y), chan: 4 (over z), seg: 2 (over x), freq: 2 (over core).
Axes of the slice: x: 2, y: 2, z: 4, core: 2. Of those that a mesh axis runs over, the one named last changes fastest.
Arguments:
- samples: bfloat16 [512, 16, 8192], P(('cable', 'chan'), 'seg'), parts along dimension 0, may hold values from -24 to 24
- live: int32 [512, 16], P('cable'), parts along dimension 0, may hold values from 0 to 1, as said below
Outputs:
- stack: bfloat16 [512, 64, 2, 256], P(('cable', 'chan', 'seg'), None, None, 'freq'), parts along dimension 0
There are 2 independent parts, one for each index of `cable`. A program takes and returns all parts, laid end to end along the dimension named above; each array names one. Nothing has to cross between parts.
Inputs may be any that keep to these rules, and one draw needn't show every extreme that they name: `live`: 1 marks a usable segment of a channel and 0 an unusable one; in every draw some channels are 0 in every segment.
All inputs are finite; a program needn't handle non-finite values.
Results may differ from a plain program's by a relative error of at most 0.006.
Values may be sent and summed in bfloat16 or wider, within the bound.
No kernel may reach another device: no remote copies, remote signals or barrier semaphores. Data moves between devices by JAX's collectives and lax.ppermute only.
A program may use at most 64 MiB of HBM per device.

v0:
```python
import math

import jax
import jax.numpy as jnp
from jax import lax
from jax.sharding import PartitionSpec as P

BINS = 256
OFFSETS = 64


EPSILON = 1e-06


def from_behind(value, axis, steps):
    count = lax.axis_size(axis)
    leading, last = (max(0, -steps), min(count, count - steps))
    return lax.ppermute(value, axis, [(source, source + steps) for source in range(leading, last)])


def dft_columns(first_bin, count, length):
    sample_index = jnp.arange(length, dtype=jnp.int32)
    bin_index = first_bin + jnp.arange(count, dtype=jnp.int32)
    phase = sample_index[:, None] * bin_index[None, :] % length
    angle = phase.astype(jnp.float32) * (2.0 * math.pi / length)
    return jnp.concatenate([jnp.cos(angle), -jnp.sin(angle)], axis=1).astype(jnp.bfloat16)


def banded(square, row_count):
    band_width = square.shape[1]
    trailing = square.shape[2:]
    flattened = square.reshape((row_count * band_width,) + trailing)
    padding = jnp.zeros((row_count,) + trailing, square.dtype)
    flattened = jnp.concatenate([flattened, padding], axis=0)
    return flattened.reshape((row_count, band_width + 1) + trailing)[:, :OFFSETS]


def cross_stack(window, live_rows, row_count):
    owned = window[:row_count]
    conjugate = jnp.array([1.0, -1.0], jnp.bfloat16).reshape(2, 1)
    real_part = jnp.einsum("iscf,jscf->ijf", owned, window, preferred_element_type=jnp.float32)
    imag_part = jnp.einsum(
        "iscf,jscf->ijf", owned * conjugate, window[:, :, ::-1], preferred_element_type=jnp.float32
    )
    pairs = jnp.dot(live_rows[:row_count], live_rows.T, preferred_element_type=jnp.float32)
    numerator = jnp.stack([banded(real_part, row_count), banded(imag_part, row_count)], axis=2)
    return (numerator / jnp.maximum(banded(pairs, row_count), 1.0)[:, :, None, None]).astype(
        jnp.bfloat16
    )


def shards(samples, live):
    chan_rows, seg_cols, length = samples.shape
    seg_count = lax.axis_size("seg")
    owned_rows = chan_rows // seg_count
    bins_dev = BINS // lax.axis_size("freq")
    lag_span = OFFSETS - 1
    chan_index = lax.axis_index("chan")
    seg_index = lax.axis_index("seg")
    dft_table = dft_columns(1 + lax.axis_index("freq") * bins_dev, bins_dev, length)
    spectra = jnp.dot(
        samples.reshape(chan_rows * seg_cols, length), dft_table, preferred_element_type=jnp.float32
    )
    spectra = spectra.reshape(chan_rows, seg_cols, 2, bins_dev)
    energy = lax.psum(jnp.sum(spectra * spectra, axis=(2, 3)), "freq")
    scaling = lax.rsqrt(energy / (2 * BINS) + EPSILON)
    usable = lax.dynamic_slice(
        live, (chan_index * chan_rows, seg_index * seg_cols), (chan_rows, seg_cols)
    ).astype(jnp.float32)
    whitened = (spectra * scaling[:, :, None, None] * usable[:, :, None, None]).astype(jnp.bfloat16)
    upper_edge = from_behind(whitened[:lag_span], "chan", -1)
    extended = jnp.concatenate([whitened, upper_edge], axis=0)
    windows = jnp.stack(
        [
            extended[target * owned_rows : target * owned_rows + owned_rows + lag_span]
            for target in range(seg_count)
        ],
        axis=0,
    )
    window = lax.all_to_all(windows, "seg", split_axis=0, concat_axis=2, tiled=True)[0]
    first_row = (chan_index * seg_count + seg_index) * owned_rows
    live_padded = jnp.concatenate([live, jnp.zeros((lag_span, live.shape[1]), jnp.int32)], axis=0)
    live_rows = lax.dynamic_slice_in_dim(live_padded, first_row, owned_rows + lag_span, 0).astype(
        jnp.bfloat16
    )
    return cross_stack(window, live_rows, owned_rows)


def solution(mesh):
    return jax.shard_map(
        shards,
        mesh=mesh,
        in_specs=(P(("cable", "chan"), "seg", None), P("cable", None)),
        out_specs=P(("cable", "chan", "seg"), None, None, "freq"),
        check_vma=False,
    )
```

profile of v0, /device:TPU:0, one launch (start us, length us, event | category | flops | bytes accessed | tf_op | source)
XLA Modules:
  0.0 78.5 jit_solution(16445167146468256540)
XLA Ops:
  0.0 0.8 dynamic-slice_convert_fusion
  0.8 0.1 copy.18
  0.9 17.0 %cosine_convert_fusion = (bf16[8192,128]{1,0:T(8,128)(2,1)S(1)}, bf16[8192,128]{1,0:T(8,128)(2,1)S(1)}) fusion(s32[128]{0:T(128)S(1)} %iota_add_fusion), kind=kLoop, calls=%fused_computation.12 | loop fusion | flops 17825792 | bytes 4194816 | tf_op jit(solution)/shard_map/convert
  17.8 5.9 %multiply_reduce_fusion = (f32[512]{0:T(512)S(1)}, f32[512,256]{0,1:T(8,128)S(1)}) fusion(bf16[64,8,8192]{2,1,0:T(8,128)(2,1)} %param.3, bf16[8192,128]{1,0:T(8,128)(2,1)S(1)} %get-tuple-element.8, bf16[8192,128]{1,0:T(8,128)(2,1)S(1)} %get-tuple-element.7), kind=kOutput, calls=%fused_computation.28 | convolution fusion | flops 2156133888 | bytes 13109248 | tf_op jit(solution)/shard_map/dot_general | solution.py:61
  23.7 0.2 copy.15
  23.9 0.1 reduce_sum.12
  24.1 2.6 %psum.7 = f32[64,8]{0,1:T(8,128)S(1)} all-reduce(f32[64,8]{0,1:T(8,128)S(1)} %copy.16), channel_id=1, replica_groups=mesh['cable'=2,'chan'=4,'seg'=2,'freq'=2] {'freq'}, use_global_device_ids=true, to_apply=%region_1.2 | all-reduce | flops 512 | bytes 4096 | tf_op jit(solution)/shard_map/psum | solution.py:65
  26.7 0.1 copy.17
  26.8 0.2 fusion.19
  27.0 1.3 %collective-permute-start = (bf16[63,8,2,128]{3,1,2,0:T(8,128)(2,1)S(1)}, bf16[63,8,2,128]{3,1,2,0:T(8,128)(2,1)S(1)}, u32[]{:S(2)}, u32[]{:S(2)}) collective-permute-start(bf16[63,8,2,128]{3,1,2,0:T(8,128)(2,1)S(1)} %slice.36), channel_id=1, source_target_pairs={{4,0},{8,4},{12,8},{5,1},{9,5},{13,9},{6,2},{10,6},{14,10},{7,3},{... | collective-permute-start | bytes 774152 | tf_op jit(solution)/shard_map/ppermute | solution.py:18
  28.3 0.1 fusion.24
  28.4 9.9 %collective-permute-done = bf16[63,8,2,128]{3,1,2,0:T(8,128)(2,1)S(1)} collective-permute-done((bf16[63,8,2,128]{3,1,2,0:T(8,128)(2,1)S(1)}, bf16[63,8,2,128]{3,1,2,0:T(8,128)(2,1)S(1)}, u32[]{:S(2)}, u32[]{:S(2)}) %collective-permute-start) | collective-permute-done | bytes 258080 | tf_op jit(solution)/shard_map/ppermute | solution.py:18
  38.4 0.9 %pad_maximum_fusion = bf16[2,95,8,2,128]{4,2,3,1,0:T(8,128)(2,1)} fusion(bf16[1,95,8,2,128]{4,2,3,1,0:T(8,128)(2,1)S(1)} %get-tuple-element.6, bf16[1,95,8,2,128]{4,2,3,1,0:T(8,128)(2,1)S(1)} %get-tuple-element.5), kind=kLoop, calls=%fused_computation.23 | loop fusion | flops 389120 | bytes 1556480 | tf_op jit(solution)/shard_map/stack | solution.py:73
  39.4 3.7 %all-to-all-start = ((bf16[2,95,8,2,128]{4,2,3,1,0:T(8,128)(2,1)}), bf16[2,95,8,2,128]{4,2,3,1,0:T(8,128)(2,1)S(1)}, u32[]{:S(2)}, u32[]{:S(2)}) async-start(bf16[2,95,8,2,128]{4,2,3,1,0:T(8,128)(2,1)} %pad_maximum_fusion), calls=%async_computation | async-start | bytes 1556480 | tf_op jit(solution)/shard_map/all_to_all | solution.py:80
  43.1 0.2 fusion.25
  43.3 0.1 reshape.41
  43.4 0.1 reshape.42
  43.5 10.2 %all-to-all-done = bf16[2,95,8,2,128]{4,2,3,1,0:T(8,128)(2,1)S(1)} async-done(((bf16[2,95,8,2,128]{4,2,3,1,0:T(8,128)(2,1)}), bf16[2,95,8,2,128]{4,2,3,1,0:T(8,128)(2,1)S(1)}, u32[]{:S(2)}, u32[]{:S(2)}) %all-to-all-start) | async-done | bytes 778272 | tf_op jit(solution)/shard_map/all_to_all | solution.py:80
  53.6 1.2 %copy.19 = bf16[1,95,2,8,2,128]{1,3,2,4,5,0:T(8,128)(2,1)S(1)} copy(bf16[1,95,2,8,2,128]{5,3,4,1,2,0:T(8,128)(2,1)S(1)} %bitcast.54) | data formatting | bytes 1556480 | tf_op jit(solution)/shard_map/all_to_all | solution.py:80
  54.9 1.5 %copy.20 = bf16[1,32,2,8,2,128]{1,3,2,4,5,0:T(8,128)(2,1)S(1)} copy(bf16[1,32,2,8,2,128]{5,3,4,1,2,0:T(8,128)(2,1)S(1)} %slice.39) | data formatting | bytes 524288 | tf_op jit(solution)/shard_map/slice | solution.py:39
  56.4 1.9 %convolution_bitcast_fusion.1 = f32[32,95,128]{1,0,2:T(8,128)} fusion(bf16[1,32,2,8,2,128]{1,3,2,4,5,0:T(8,128)(2,1)S(1)} %copy.20, bf16[1,95,2,8,2,128]{1,3,2,4,5,0:T(8,128)(2,1)S(1)} %copy.19), kind=kOutput, calls=%fused_computation.19 | convolution fusion | flops 24903680 | bytes 2596864 | tf_op jit(solution)/shard_map/iscf,jscf->ijf/dot_general | solution.py:41
  58.2 3.4 %reshape.45 = f32[3040,128]{0,1:T(8,128)} reshape(f32[32,95,128]{1,0,2:T(8,128)} %convolution_bitcast_fusion.1) | data formatting | bytes 3112960 | tf_op jit(solution)/shard_map/reshape | solution.py:32
  61.6 3.0 %copy.25 = f32[3040,128]{1,0:T(8,128)} copy(f32[3040,128]{0,1:T(8,128)} %reshape.45) | data formatting | bytes 3112960 | tf_op jit(solution)/shard_map/reshape | solution.py:32
  64.7 1.5 %concatenate.21 = f32[3072,128]{1,0:T(8,128)S(1)} pad(f32[3040,128]{1,0:T(8,128)} %copy.25, f32[]{:T(128)} %constant.17.clone.1), padding=0_32x0_0 | pad | bytes 3129348 | tf_op jit(solution)/shard_map/concatenate | solution.py:34
  66.2 1.1 %slice.40 = f32[32,64,128]{2,1,0:T(8,128)} slice(f32[32,96,128]{2,1,0:T(8,128)S(1)} %bitcast.52), slice={[0:32], [0:64], [0:128]} | slice | bytes 2097152 | tf_op jit(solution)/shard_map/slice | solution.py:35
  67.3 1.1 %rev.3 = bf16[95,16,2,128]{0,1,2,3:T(8,128)(2,1)} reverse(bf16[95,16,2,128]{0,1,2,3:T(8,128)(2,1)S(1)} %bitcast.50), dimensions={2} | reverse | bytes 1556480 | tf_op jit(solution)/shard_map/rev | solution.py:43
  68.4 1.8 %convolution_bitcast_fusion = f32[32,95,128]{1,0,2:T(8,128)S(1)} fusion(bf16[95,16,2,128]{0,1,2,3:T(8,128)(2,1)} %rev.3, bf16[1,32,2,8,2,128]{1,3,2,4,5,0:T(8,128)(2,1)S(1)} %copy.20, bf16[2]{0:T(256)(128)(2,1)S(1)} %copy-done.2), kind=kOutput, calls=%fused_computation.18 | convolution fusion | flops 25034752 | bytes 2596868 | tf_op jit(solution)/shard_map/iscf,jscf->ijf/dot_general | solution.py:42
  70.2 2.8 %reshape.46 = f32[3040,128]{0,1:T(8,128)} reshape(f32[32,95,128]{1,0,2:T(8,128)S(1)} %convolution_bitcast_fusion) | data formatting | bytes 3112960 | tf_op jit(solution)/shard_map/reshape | solution.py:32
  73.0 2.0 %copy.26 = f32[3040,128]{1,0:T(8,128)S(1)} copy(f32[3040,128]{0,1:T(8,128)} %reshape.46) | data formatting | bytes 3112960 | tf_op jit(solution)/shard_map/reshape | solution.py:32
  74.9 0.1 concatenate.22
  75.1 0.1 slice.41
  75.2 3.3 %fusion.11 = bf16[32,64,2,128]{3,2,1,0:T(2,128)(2,1)} fusion(f32[32,64,1,128]{3,2,1,0:T(1,128)S(1)} %bitcast.56, f32[32,64,1,128]{3,2,1,0:T(1,128)S(1)} %bitcast.55, f32[32,64]{1,0:T(8,128)S(1)} %slice_maximum_fusion), kind=kLoop, calls=%fused_computation.17 | loop fusion | flops 1572864 | bytes 3153920 | tf_op jit(solution)/shard_map/convert_element_type | solution.py:47
  (14 shorter events, 0.2 us)
Async XLA Ops:
  17.8 10.5 %copy-start.1 = (s32[256,16]{0,1:T(8,128)S(1)}, s32[256,16]{0,1:T(8,128)}, u32[]{:S(2)}) copy-start(s32[256,16]{0,1:T(8,128)} %param.4) | copy-start | bytes 49156
  27.0 11.3 %collective-permute-start = (bf16[63,8,2,128]{3,1,2,0:T(8,128)(2,1)S(1)}, bf16[63,8,2,128]{3,1,2,0:T(8,128)(2,1)S(1)}, u32[]{:S(2)}, u32[]{:S(2)}) collective-permute-start(bf16[63,8,2,128]{3,1,2,0:T(8,128)(2,1)S(1)} %slice.36), channel_id=1, source_target_pairs={{4,0},{8,4},{12,8},{5,1},{9,5},{13,9},{6,2},{10,6},{14,10},{7,3},{... | collective-permute-start | bytes 774152 | tf_op jit(solution)/shard_map/ppermute | solution.py:18
  39.4 14.3 %all-to-all-start = ((bf16[2,95,8,2,128]{4,2,3,1,0:T(8,128)(2,1)}), bf16[2,95,8,2,128]{4,2,3,1,0:T(8,128)(2,1)S(1)}, u32[]{:S(2)}, u32[]{:S(2)}) async-start(bf16[2,95,8,2,128]{4,2,3,1,0:T(8,128)(2,1)} %pad_maximum_fusion), calls=%async_computation | async-start | bytes 1556480 | tf_op jit(solution)/shard_map/all_to_all | solution.py:80
  64.7 3.7 %copy-start.2 = (bf16[2]{0:T(256)(128)(2,1)S(1)}, bf16[2]{0:T(256)(128)(2,1)}, u32[]{:S(2)}) copy-start(bf16[2]{0:T(256)(128)(2,1)} %constant.61.clone) | copy-start | bytes 16
  73.0 2.2 %copy-start = (f32[32,64,128]{2,1,0:T(8,128)S(1)}, f32[32,64,128]{2,1,0:T(8,128)}, u32[]{:S(2)}) copy-start(f32[32,64,128]{2,1,0:T(8,128)} %slice.40) | copy-start | bytes 3145732
where the time goes:
time: 78.9 us; the launch traced here: 78.5 us
  other arithmetic  22.3 us (28%)
  waiting for transfers between devices  20.1 us (25%)
  local copies, waits for them, and re-layouts  18.5 us (23%)
  matrix products  9.72 us (12%)
  starting transfers between devices  5.01 us (6%)
  blocking collectives  2.62 us (3%)
    another operation x1, other arithmetic  17 us
    reshape x5, local copies, waits for them, and re-layouts, banded(): flattened = square.reshape((row_count * band_width,) + trailing)  11.3 us
    all_to_all x1, waiting for transfers between devices, shards(): lax.all_to_all(windows, 'seg', split_axis=0, concat_axis=2, tiled=True)[0]  10.2 us
    ppermute x1, waiting for transfers between devices, from_behind(): lax.ppermute(value, axis, [(source, source + steps) for source in range(l...  9.95 us
    dot_general x1, matrix products, shards(): jnp.dot(samples.reshape(chan_rows * seg_cols, length), dft_table, preferr...  5.88 us
    all_to_all x1, starting transfers between devices, shards(): lax.all_to_all(windows, 'seg', split_axis=0, concat_axis=2, tiled=True)[0]  3.71 us
    convert_element_type x1, other arithmetic, cross_stack(): (numerator / jnp.maximum(banded(pairs, row_count), 1.0)[:, :, None, None]...  3.3 us
    psum x1, blocking collectives, shards(): energy = lax.psum(jnp.sum(spectra * spectra, axis=(2, 3)), 'freq')  2.62 us
  transfers between devices with their start and end apart: 2, of which 2 were waited for; matrix products, arithmetic and copies ran while one was open for 1% of the time, Pallas kernels for 0%

commit v1 on v0

v1 whole, which is shorter than its diff:
```python
import functools
import math

import jax
import jax.numpy as jnp
import numpy as np
from jax import lax
from jax.experimental import pallas as pl
from jax.experimental.pallas import tpu as pltpu
from jax.sharding import PartitionSpec as P

BINS = 256
OFFSETS = 64
EPSILON = 1e-06
QUARTERS = 4
BASE = 16
LANES = 128
VMEM = pl.BlockSpec(memory_space=pltpu.VMEM)
ANY = pl.BlockSpec(memory_space=pl.ANY)


def rotations(length):
    quarter = length // QUARTERS
    doublings = int(math.log2(quarter // BASE))
    times = np.concatenate(
        [np.arange(BASE), BASE * 2 ** np.arange(doublings), quarter * np.arange(QUARTERS)]
    )
    times = np.concatenate([times, np.zeros(-len(times) % 8, np.int64)])
    angle = (times[:, None] * (1 + np.arange(BINS))[None, :] % length) * (2.0 * math.pi / length)
    table = np.stack([np.cos(angle), np.sin(angle)])
    return np.where(np.abs(table) < 1e-12, 0.0, table).astype(np.float32), doublings


def dft_kernel(doublings, samples, live_t, trig, mine_out, other_out, block, rot, cos_t, sin_t, table, spec, scale, live_col, sem):
    rows = spec.shape[1]
    seg_cols, quarter = mine_out.shape[0] // 2, block.shape[2]
    chans = rows // seg_cols
    freq = lax.axis_index("freq")
    seg = lax.axis_index("seg")
    half = BINS // 2
    row0 = pl.multiple_of(freq * rows, rows)
    rot_copy = pltpu.make_async_copy(trig, rot, sem.at[QUARTERS])
    rot_copy.start()
    copies = []
    for q in range(QUARTERS):
        copy = pltpu.make_async_copy(
            samples.at[pl.ds(row0, rows), pl.ds(q * quarter, quarter)], block.at[q], sem.at[q]
        )
        copy.start()
        copies.append(copy)
    live_col[...] = live_t[...].T.astype(jnp.float32)
    rot_copy.wait()
    cos_t[0:BASE] = rot[0, 0:BASE]
    sin_t[0:BASE] = rot[1, 0:BASE]
    done = BASE
    for step in range(doublings):
        ca, sa = rot[0, BASE + step : BASE + step + 1], rot[1, BASE + step : BASE + step + 1]
        c, s = cos_t[0:done], sin_t[0:done]
        cos_t[done : 2 * done] = c * ca - s * sa
        sin_t[done : 2 * done] = s * ca + c * sa
        done *= 2
    for h in range(2):
        table[:, h * BINS : h * BINS + half] = cos_t[:, h * half : (h + 1) * half].astype(jnp.bfloat16)
        table[:, h * BINS + half : (h + 1) * BINS] = (-sin_t[:, h * half : (h + 1) * half]).astype(jnp.bfloat16)
    first = BASE + doublings
    for q in range(QUARTERS):
        if q % 2 == 0:
            copies[q].wait()
            copies[q + 1].wait()
        part = jnp.dot(block[q], table[...], preferred_element_type=jnp.float32)
        for h in range(2):
            re = part[:, h * BINS : h * BINS + half]
            im = part[:, h * BINS + half : (h + 1) * BINS]
            if q == 0:
                spec[2 * h], spec[2 * h + 1] = re, im
                continue
            al = rot[0, first + q : first + q + 1, h * half : (h + 1) * half]
            be = rot[1, first + q : first + q + 1, h * half : (h + 1) * half]
            spec[2 * h] += re * al + im * be
            spec[2 * h + 1] += im * al - re * be
    squares = jnp.zeros((rows, LANES), jnp.float32)
    for tile in range(4):
        squares += spec[tile] * spec[tile]
    energy = jnp.sum(squares, axis=1, keepdims=True)
    scale[...] = jnp.broadcast_to(lax.rsqrt(energy / (2 * BINS) + EPSILON), scale.shape)
    first_chan = pl.multiple_of(lax.axis_index("chan") * (chans * lax.axis_size("freq")) + freq * chans, chans)
    live = live_col[pl.ds(first_chan, chans), :]
    column = lax.broadcasted_iota(jnp.int32, live.shape, 1)
    for s in range(seg_cols):
        usable = jnp.sum(jnp.where(column == seg * seg_cols + s, live, 0.0), axis=1, keepdims=True)
        factor = scale[pl.ds(s, chans, stride=seg_cols), :]
        for r in range(2):
            for out, h in ((mine_out, freq), (other_out, 1 - freq)):
                value = spec[2 * h + r, pl.ds(s, chans, stride=seg_cols), :]
                out[2 * s + r] = (value * factor * usable).astype(jnp.bfloat16)


def whitened_half(samples, live):
    chan_rows, seg_cols, length = samples.shape
    rows = chan_rows * seg_cols // 2
    trig, doublings = rotations(length)
    quarter = length // QUARTERS
    out = jax.ShapeDtypeStruct((2 * seg_cols, chan_rows // 2, BINS // 2), jnp.bfloat16)
    return pl.pallas_call(
        functools.partial(dft_kernel, doublings),
        in_specs=[ANY, VMEM, ANY],
        out_specs=[VMEM, VMEM],
        out_shape=[out, out],
        scratch_shapes=[
            pltpu.VMEM((QUARTERS, rows, quarter), jnp.bfloat16),
            pltpu.VMEM(trig.shape, jnp.float32),
            pltpu.VMEM((quarter, BINS), jnp.float32),
            pltpu.VMEM((quarter, BINS), jnp.float32),
            pltpu.VMEM((quarter, 2 * BINS), jnp.bfloat16),
            pltpu.VMEM((2 * BINS // LANES, rows, LANES), jnp.float32),
            pltpu.VMEM((rows, LANES), jnp.float32),
            pltpu.VMEM((live.shape[0], live.shape[1]), jnp.float32),
            pltpu.SemaphoreType.DMA((QUARTERS + 1,)),
        ],
        compiler_params=pltpu.CompilerParams(vmem_limit_bytes=48 << 20),
        cost_estimate=pl.CostEstimate(flops=4 * rows * length * BINS, bytes_accessed=2 * rows * length, transcendentals=0),
        name="dft_whiten",
    )(samples.reshape(chan_rows * seg_cols, length), live.T, jnp.asarray(trig))


def cross_kernel(load, owned, inv_t, *refs):
    out, rows_re, rows_im, rows_sum, rows_dif, pairs = refs[-6:]
    load(refs[:-6], rows_re, rows_im)
    segs, width = rows_re.shape[0], rows_re.shape[1]
    for s in range(segs):
        re, im = rows_re[s], rows_im[s]
        rows_sum[s] = re + im
        rows_dif[s] = re - im
    blocks = OFFSETS // 8
    lane = lax.broadcasted_iota(jnp.int32, inv_t.shape, 1)

    def channel(i, carry):
        k1 = [None] * blocks
        k2 = [None] * blocks
        k3 = [None] * blocks
        for s in range(segs):
            a_re = rows_re[s, pl.ds(i, 8, stride=0), :]
            a_sum = rows_sum[s, pl.ds(i, 8, stride=0), :]
            a_dif = rows_dif[s, pl.ds(i, 8, stride=0), :]
            for m in range(blocks):
                at = pl.ds(i + 8 * m, 8)
                t1 = a_re * rows_sum[s, at, :]
                t2 = a_dif * rows_im[s, at, :]
                t3 = a_sum * rows_re[s, at, :]
                k1[m] = t1 if s == 0 else k1[m] + t1
                k2[m] = t2 if s == 0 else k2[m] + t2
                k3[m] = t3 if s == 0 else k3[m] + t3
        inverse = jnp.sum(jnp.where(lane == i, inv_t[...], 0.0), axis=1, keepdims=True)
        for m in range(blocks):
            inv = inverse[8 * m : 8 * m + 8]
            pairs[pl.ds(16 * m, 8, stride=2), :] = (k1[m] - k2[m]) * inv
            pairs[pl.ds(16 * m + 1, 8, stride=2), :] = (k1[m] - k3[m]) * inv
        out[i] = pairs[...].astype(jnp.bfloat16)
        return carry

    lax.fori_loop(0, owned, channel, 0)


def cross_stack(load, arrays, inv_t, owned, segs, width):
    scratch = pltpu.VMEM((segs, width, LANES), jnp.float32)
    bins = arrays[0].shape[-1]
    out = pl.pallas_call(
        functools.partial(cross_kernel, load, owned),
        in_specs=[VMEM] * (1 + len(arrays)),
        out_specs=VMEM,
        out_shape=jax.ShapeDtypeStruct((owned, 2 * OFFSETS, bins), jnp.bfloat16),
        scratch_shapes=[scratch] * 4 + [pltpu.VMEM((2 * OFFSETS, LANES), jnp.float32)],
        compiler_params=pltpu.CompilerParams(vmem_limit_bytes=48 << 20),
        cost_estimate=pl.CostEstimate(flops=8 * owned * OFFSETS * segs * bins, bytes_accessed=owned * OFFSETS * bins * 4, transcendentals=0),
        name="cross",
    )(inv_t, *arrays)
    return out.reshape(owned, OFFSETS, 2, bins)


def inverse_pairs(live, first_row, owned):
    width = owned + OFFSETS
    padded = jnp.concatenate([live, jnp.zeros((OFFSETS, live.shape[1]), live.dtype)], axis=0)
    rows = lax.dynamic_slice_in_dim(padded, first_row, width, 0).astype(jnp.bfloat16)
    square = jnp.dot(rows, rows[:owned].T, preferred_element_type=jnp.float32)
    flat = square.T.reshape(owned * width)
    flat = jnp.concatenate([flat, jnp.zeros((owned,), flat.dtype)])
    band = flat.reshape(owned, width + 1)[:, :OFFSETS]
    return 1.0 / jnp.maximum(band, 1.0).T


def split(value, segs, rows_re, rows_im, first_seg, first_row):
    count = value.shape[1]
    for s in range(segs):
        rows_re[first_seg + s, first_row : first_row + count, :] = value[2 * s].astype(jnp.float32)
        rows_im[first_seg + s, first_row : first_row + count, :] = value[2 * s + 1].astype(jnp.float32)


def load_direct(segs, unit, refs, rows_re, rows_im):
    low, high, both, far, near, next_high = refs
    x = lax.axis_index("seg")
    put = lambda value, group, row: split(value, segs, rows_re, rows_im, group * segs, row * unit)
    for s in range(2 * segs):
        rows_re[s, 3 * unit :, :] = jnp.zeros((8, LANES), jnp.float32)
        rows_im[s, 3 * unit :, :] = jnp.zeros((8, LANES), jnp.float32)

    @pl.when(x == 0)
    def _():
        put(low[...], 0, 0)
        put(high[...], 0, 1)
        put(near[...], 0, 2)
        put(both[...], 1, 0)
        put(far[...], 1, 2)

    @pl.when(x == 1)
    def _():
        put(high[...], 0, 0)
        put(near[...], 0, 1)
        put(next_high[...], 0, 2)
        put(far[...], 1, 0)
        put(both[...], 1, 1)


def direct(low, high, live, unit):
    chan, z = lax.axis_size("chan"), lax.axis_index("chan")
    x = lax.axis_index("seg")
    at = lambda block, group: 2 * block + group
    send = lambda value, pairs: lax.ppermute(value, ("chan", "seg"), pairs)
    to_side = [(at(b, 1), at(b, 0)) for b in range(chan)]
    to_corner = [(at(b, 0), at(b - 1, 1)) for b in range(1, chan)]
    from_side = [(at(b, 0), at(b, 1)) for b in range(chan)]
    from_corner = [(at(b, 1), at(b - 1, 0)) for b in range(1, chan)]
    below = [(at(b, g), at(b - 1, g)) for b in range(1, chan) for g in range(2)]
    below_one = [(at(b, 1), at(b - 1, 1)) for b in range(1, chan)]
    both = send(jnp.concatenate([low, high], axis=1), to_side + to_corner)
    far = send(jnp.where(x == 0, high, low), from_side + from_corner)
    near = send(low, below)
    next_high = send(high, below_one)
    segs = low.shape[0] // 2
    inv_t = inverse_pairs(live, (2 * z + x) * unit, unit)
    return cross_stack(
        functools.partial(load_direct, segs, unit),
        [low, high, both, far, near, next_high],
        inv_t, unit, 2 * segs, 3 * unit + 8,
    )


def load_window(segs, width, refs, rows_re, rows_im):
    (window,) = refs
    for g in range(window.shape[0]):
        split(window[g], segs, rows_re, rows_im, g * segs, 0)
    for s in range(rows_re.shape[0]):
        rows_re[s, width:, :] = jnp.zeros((8, LANES), jnp.float32)
        rows_im[s, width:, :] = jnp.zeros((8, LANES), jnp.float32)


def gathered(low, high, live, owned):
    groups, chan = lax.axis_size("seg"), lax.axis_size("chan")
    own = jnp.concatenate([low, high], axis=1)
    above = lax.ppermute(own[:, :OFFSETS], "chan", [(b, b - 1) for b in range(1, chan)])
    extended = jnp.concatenate([own, above], axis=1)
    width = owned + OFFSETS
    windows = jnp.stack([extended[:, t * owned : t * owned + width] for t in range(groups)])
    window = lax.all_to_all(windows, "seg", split_axis=0, concat_axis=0, tiled=True)
    segs = low.shape[0] // 2
    first_row = (lax.axis_index("chan") * groups + lax.axis_index("seg")) * owned
    inv_t = inverse_pairs(live, first_row, owned)
    return cross_stack(
        functools.partial(load_window, segs, width), [window], inv_t, owned, groups * segs, width + 8
    )


def shards(samples, live):
    mine, other = whitened_half(samples, live)
    theirs = lax.ppermute(other, "freq", [(0, 1), (1, 0)])
    freq = lax.axis_index("freq")
    low = jnp.where(freq == 0, mine, theirs)
    high = jnp.where(freq == 0, theirs, mine)
    groups = lax.axis_size("seg")
    owned = samples.shape[0] // groups
    step = direct if groups == 2 and owned == OFFSETS // 2 else gathered
    return step(low, high, live, owned)


def solution(mesh):
    return jax.shard_map(
        shards,
        mesh=mesh,
        in_specs=(P(("cable", "chan"), "seg", None), P("cable", None)),
        out_specs=P(("cable", "chan", "seg"), None, None, "freq"),
        check_vma=False,
    )
```

time: 78.9 us -> 30.6 us (0.39)
  other arithmetic: 22.3 us -> 0.14 us
  local copies, waits for them, and re-layouts: 18.5 us -> 1.82 us
  waiting for transfers between devices: 20.1 us -> 8.96 us
  matrix products: 9.72 us -> 0.17 us
  Pallas kernels: 0 us -> 9.34 us
  starting transfers between devices: 5.01 us -> 9.8 us
  blocking collectives: 2.62 us -> 0 us
    another operation x3 -> x0, other arithmetic: 18 us -> none
    reshape x6 -> x2, local copies, waits for them, and re-layouts: 11.3 us -> 0.18 us  [the longest x1 0.11 us: inverse_pairs(): band = flat.reshape(owned, width + 1)[:, :OFFSETS]]
    all_to_all x1 -> x0, waiting for transfers between devices: 10.2 us -> none  [shards(): lax.all_to_all(windows, 'seg', split_axis=0, concat_axis=2, tiled=True)[0]]
    dot_general x4 -> x1, matrix products: 9.72 us -> 0.17 us  [inverse_pairs(): square = jnp.dot(rows, rows[:owned].T, preferred_element_type=jnp.float32)]
    pallas_call x0 -> x2, Pallas kernels: none -> 9.34 us  [the longest x1 4.97 us: cross_stack(): pl.pallas_call(functools.partial(cross_kernel, load, owned), in_specs=[VM...]
    ppermute x1 -> x5, starting transfers between devices: 1.29 us -> 9.8 us  [the longest x4 9.24 us: direct(): send = lambda value, pairs: lax.ppermute(value, ('chan', 'seg'), pairs)]
    convert_element_type x4 -> x1, other arithmetic: 4.34 us -> 0.08 us  [inverse_pairs(): lax.dynamic_slice_in_dim(padded, first_row, width, 0).astype(jnp.bfloat16)]
    all_to_all x1 -> x0, starting transfers between devices: 3.71 us -> none  [shards(): lax.all_to_all(windows, 'seg', split_axis=0, concat_axis=2, tiled=True)[0]]
  transfers between devices with their start and end apart: 2 -> 5, of which waited for: 2 -> 2; matrix products, arithmetic and copies ran while one was open for 1% -> 2% of each run, Pallas kernels for 0% -> 0%
where the time goes in v1:
time: 30.6 us; the launch traced here: 30.3 us
  starting transfers between devices  9.8 us (32%)
  Pallas kernels  9.34 us (31%)
  waiting for transfers between devices  8.96 us (29%)
  local copies, waits for them, and re-layouts  1.82 us (6%)
    ppermute x4, starting transfers between devices, direct(): send = lambda value, pairs: lax.ppermute(value, ('chan', 'seg'), pairs)  9.24 us
    ppermute x4, waiting for transfers between devices, direct(): send = lambda value, pairs: lax.ppermute(value, ('chan', 'seg'), pairs)  8.05 us
    pallas_call x1, Pallas kernels, cross_stack(): pl.pallas_call(functools.partial(cross_kernel, load, owned), in_specs=[VM...  4.97 us
    pallas_call x1, Pallas kernels, whitened_half(): pl.pallas_call(functools.partial(dft_kernel, doublings), in_specs=[ANY, V...  4.36 us
    unnamed x7, local copies, waits for them, and re-layouts  1.64 us
    ppermute x1, waiting for transfers between devices, shards(): theirs = lax.ppermute(other, 'freq', [(0, 1), (1, 0)])  0.91 us
  transfers between devices with their start and end apart: 5, of which 2 were waited for; matrix products, arithmetic and copies ran while one was open for 2% of the time, Pallas kernels for 0%

profile of v1, /device:TPU:0, one launch (start us, length us, event | category | flops | bytes accessed | tf_op | source)
XLA Modules:
  0.0 30.3 jit_solution(230602481821501524)
XLA Ops:
  0.0 0.0 copy-start
  0.0 0.8 %copy-done = f32[2,32,256]{2,1,0:T(8,128)S(1)} copy-done((f32[2,32,256]{2,1,0:T(8,128)S(1)}, f32[2,32,256]{2,1,0:T(8,128)}, u32[]{:S(2)}) %copy-start) | copy-done | bytes 65560
  0.8 0.0 copy-start.1
  0.8 0.7 %copy-done.1 = s32[256,16]{0,1:T(8,128)S(1)} copy-done((s32[256,16]{0,1:T(8,128)S(1)}, s32[256,16]{0,1:T(8,128)}, u32[]{:S(2)}) %copy-start.1) | copy-done | bytes 16408
  1.6 0.0 copy-start.2
  1.6 4.4 %dft_whiten.1 = (bf16[16,32,128]{2,1,0:T(8,128)(2,1)S(1)}, bf16[16,32,128]{2,1,0:T(8,128)(2,1)S(1)}) custom-call(bf16[512,8192]{1,0:T(8,128)(2,1)} %bitcast.8, s32[16,256]{1,0:T(8,128)S(1)} %bitcast.7, f32[2,32,256]{2,1,0:T(8,128)S(1)} %copy-done), custom_call_target="tpu_custom_call" | custom-call | flops 2147483648 | bytes 4194304 | tf_op jit(solution)/shard_map/dft_whiten/pallas_call | solution.py:104
  5.9 0.6 %collective-permute-start = (bf16[16,32,128]{2,1,0:T(8,128)(2,1)S(1)}, bf16[16,32,128]{2,1,0:T(8,128)(2,1)S(1)}, u32[]{:S(2)}, u32[]{:S(2)}) collective-permute-start(bf16[16,32,128]{2,1,0:T(8,128)(2,1)S(1)} %get-tuple-element.8), channel_id=1, source_target_pairs={{0,1},{1,0},{2,3},{3,2},{4,5},{5,4},{6,7},{7,6},{8,9},{9,8},{10,11... | collective-permute-start | bytes 393224 | tf_op jit(solution)/shard_map/ppermute | solution.py:274
  6.5 0.0 copy-done.2
  6.5 0.1 fusion
  6.6 0.9 %collective-permute-done = bf16[16,32,128]{2,1,0:T(8,128)(2,1)S(1)} collective-permute-done((bf16[16,32,128]{2,1,0:T(8,128)(2,1)S(1)}, bf16[16,32,128]{2,1,0:T(8,128)(2,1)S(1)}, u32[]{:S(2)}, u32[]{:S(2)}) %collective-permute-start) | collective-permute-done | bytes 131104 | tf_op jit(solution)/shard_map/ppermute | solution.py:274
  7.5 1.3 %collective-permute-start.1 = (bf16[16,64,128]{2,1,0:T(8,128)(2,1)S(1)}, bf16[16,64,128]{2,1,0:T(8,128)(2,1)S(1)}, u32[]{:S(2)}, u32[]{:S(2)}) collective-permute-start(bf16[16,64,128]{2,1,0:T(8,128)(2,1)S(1)} %pad_maximum_fusion), channel_id=1, source_target_pairs={{2,0},{6,4},{10,8},{14,12},{4,2},{8,6},{12,10},{3,1},{7,5},{11,9},... | collective-permute-start | bytes 786440 | tf_op jit(solution)/shard_map/ppermute | solution.py:227
  8.8 0.2 fusion.1
  9.0 0.1 reshape.12
  9.1 0.1 reshape.13
  9.2 0.1 copy.5
  9.3 0.7 %collective-permute-start.4 = (bf16[16,32,128]{2,1,0:T(8,128)(2,1)S(1)}, bf16[16,32,128]{2,1,0:T(8,128)(2,1)S(1)}, u32[]{:S(2)}, u32[]{:S(2)}) collective-permute-start(bf16[16,32,128]{2,1,0:T(8,128)(2,1)S(1)} %get-tuple-element.10.refs_1_), channel_id=1, source_target_pairs={{6,2},{10,6},{14,10},{7,3},{11,7},{15,11},{22,18},{26,22},{30,26},... | collective-permute-start | bytes 393224 | tf_op jit(solution)/shard_map/ppermute | solution.py:227
  10.0 1.3 %collective-permute-start.3 = (bf16[16,32,128]{2,1,0:T(8,128)(2,1)S(1)}, bf16[16,32,128]{2,1,0:T(8,128)(2,1)S(1)}, u32[]{:S(2)}, u32[]{:S(2)}) collective-permute-start(bf16[16,32,128]{2,1,0:T(8,128)(2,1)S(1)} %get-tuple-element.11.refs_0_), channel_id=1, source_target_pairs={{4,0},{6,2},{8,4},{10,6},{12,8},{14,10},{5,1},{7,3},{9,5},{11,7},{... | collective-permute-start | bytes 393224 | tf_op jit(solution)/shard_map/ppermute | solution.py:227
  11.3 6.0 %collective-permute-start.2 = (bf16[16,32,128]{2,1,0:T(8,128)(2,1)S(1)}, bf16[16,32,128]{2,1,0:T(8,128)(2,1)S(1)}, u32[]{:S(2)}, u32[]{:S(2)}) collective-permute-start(bf16[16,32,128]{2,1,0:T(8,128)(2,1)S(1)} %get-tuple-element.9), channel_id=1, source_target_pairs={{0,2},{4,6},{8,10},{12,14},{6,0},{10,4},{14,8},{1,3},{5,7},{9,11},... | collective-permute-start | bytes 393224 | tf_op jit(solution)/shard_map/ppermute | solution.py:227
  17.3 8.0 %collective-permute-done.2.refs_3_ = bf16[16,32,128]{2,1,0:T(8,128)(2,1)S(1)} collective-permute-done((bf16[16,32,128]{2,1,0:T(8,128)(2,1)S(1)}, bf16[16,32,128]{2,1,0:T(8,128)(2,1)S(1)}, u32[]{:S(2)}, u32[]{:S(2)}) %collective-permute-start.2) | collective-permute-done | bytes 131104 | tf_op jit(solution)/shard_map/ppermute | solution.py:227
  25.3 0.0 collective-permute-done.4.refs_5_
  25.3 0.0 collective-permute-done.3.refs_4_
  25.3 0.0 collective-permute-done.1.refs_2_
  25.3 5.0 %cross.1 = bf16[32,128,128]{2,1,0:T(8,128)(2,1)} custom-call(f32[64,32]{1,0:T(8,128)S(1)} %divide_bitcast_fusion.inv_t, bf16[16,32,128]{2,1,0:T(8,128)(2,1)S(1)} %get-tuple-element.11.refs_0_, bf16[16,32,128]{2,1,0:T(8,128)(2,1)S(1)} %get-tuple-element.10.refs_1_, bf16[16,64,128]{2,1,0:T(8,128)(2,1)S(1)} %collective-permute-done.1.refs_2_, ...), custom_call_target="tpu_custom_call" | custom-call | flops 33554432 | bytes 1048576 | tf_op jit(solution)/shard_map/cross/pallas_call | solution.py:167
  (4 shorter events, 0.1 us)
Async XLA Ops:
  0.0 0.8 %copy-start = (f32[2,32,256]{2,1,0:T(8,128)S(1)}, f32[2,32,256]{2,1,0:T(8,128)}, u32[]{:S(2)}) copy-start(f32[2,32,256]{2,1,0:T(8,128)} %constant.27.clone.trig) | copy-start | bytes 196612
  0.8 0.7 %copy-start.1 = (s32[256,16]{0,1:T(8,128)S(1)}, s32[256,16]{0,1:T(8,128)}, u32[]{:S(2)}) copy-start(s32[256,16]{0,1:T(8,128)} %param.4) | copy-start | bytes 49156
  1.6 4.9 %copy-start.2 = (s32[256,16]{0,1:T(8,128)S(1)}, s32[256,16]{0,1:T(8,128)}, u32[]{:S(2)}) copy-start(s32[256,16]{0,1:T(8,128)} %param.4) | copy-start | bytes 49156
  5.9 1.5 %collective-permute-start = (bf16[16,32,128]{2,1,0:T(8,128)(2,1)S(1)}, bf16[16,32,128]{2,1,0:T(8,128)(2,1)S(1)}, u32[]{:S(2)}, u32[]{:S(2)}) collective-permute-start(bf16[16,32,128]{2,1,0:T(8,128)(2,1)S(1)} %get-tuple-element.8), channel_id=1, source_target_pairs={{0,1},{1,0},{2,3},{3,2},{4,5},{5,4},{6,7},{7,6},{8,9},{9,8},{10,11... | collective-permute-start | bytes 393224 | tf_op jit(solution)/shard_map/ppermute | solution.py:274
  7.5 17.8 %collective-permute-start.1 = (bf16[16,64,128]{2,1,0:T(8,128)(2,1)S(1)}, bf16[16,64,128]{2,1,0:T(8,128)(2,1)S(1)}, u32[]{:S(2)}, u32[]{:S(2)}) collective-permute-start(bf16[16,64,128]{2,1,0:T(8,128)(2,1)S(1)} %pad_maximum_fusion), channel_id=1, source_target_pairs={{2,0},{6,4},{10,8},{14,12},{4,2},{8,6},{12,10},{3,1},{7,5},{11,9},... | collective-permute-start | bytes 786440 | tf_op jit(solution)/shard_map/ppermute | solution.py:227
  9.3 16.0 %collective-permute-start.4 = (bf16[16,32,128]{2,1,0:T(8,128)(2,1)S(1)}, bf16[16,32,128]{2,1,0:T(8,128)(2,1)S(1)}, u32[]{:S(2)}, u32[]{:S(2)}) collective-permute-start(bf16[16,32,128]{2,1,0:T(8,128)(2,1)S(1)} %get-tuple-element.10.refs_1_), channel_id=1, source_target_pairs={{6,2},{10,6},{14,10},{7,3},{11,7},{15,11},{22,18},{26,22},{30,26},... | collective-permute-start | bytes 393224 | tf_op jit(solution)/shard_map/ppermute | solution.py:227
  10.0 15.4 %collective-permute-start.3 = (bf16[16,32,128]{2,1,0:T(8,128)(2,1)S(1)}, bf16[16,32,128]{2,1,0:T(8,128)(2,1)S(1)}, u32[]{:S(2)}, u32[]{:S(2)}) collective-permute-start(bf16[16,32,128]{2,1,0:T(8,128)(2,1)S(1)} %get-tuple-element.11.refs_0_), channel_id=1, source_target_pairs={{4,0},{6,2},{8,4},{10,6},{12,8},{14,10},{5,1},{7,3},{9,5},{11,7},{... | collective-permute-start | bytes 393224 | tf_op jit(solution)/shard_map/ppermute | solution.py:227
  11.3 14.1 %collective-permute-start.2 = (bf16[16,32,128]{2,1,0:T(8,128)(2,1)S(1)}, bf16[16,32,128]{2,1,0:T(8,128)(2,1)S(1)}, u32[]{:S(2)}, u32[]{:S(2)}) collective-permute-start(bf16[16,32,128]{2,1,0:T(8,128)(2,1)S(1)} %get-tuple-element.9), channel_id=1, source_target_pairs={{0,2},{4,6},{8,10},{12,14},{6,0},{10,4},{14,8},{1,3},{5,7},{9,11},... | collective-permute-start | bytes 393224 | tf_op jit(solution)/shard_map/ppermute | solution.py:227

commit v2 on v1

v2 whole, which is shorter than its diff:
```python
import functools
import math

import jax
import jax.numpy as jnp
from jax import lax
from jax.experimental import pallas as pl
from jax.experimental.pallas import tpu as pltpu
from jax.sharding import PartitionSpec as P


BINS = 256
OFFSETS = 64
EPSILON = 1e-06
QUARTERS = 4
BASE = 16
STEP = 32
LANES = 128
VMEM = pl.BlockSpec(memory_space=pltpu.VMEM)
HBM = pl.BlockSpec(memory_space=pltpu.HBM)


def dft_kernel(length, doublings, samples, mine_out, other_out, block, rot, cos_t, sin_t, table, spec, scale, sem):
    rows = spec.shape[1]
    seg_cols, quarter = mine_out.shape[0] // 2, block.shape[2]
    chans = rows // seg_cols
    freq = lax.axis_index("freq")
    half = BINS // 2
    row0 = pl.multiple_of(freq * rows, rows)
    copies = []
    for q in range(QUARTERS):
        copy = pltpu.make_async_copy(
            samples.at[pl.ds(row0, rows), pl.ds(q * quarter, quarter)], block.at[q], sem.at[q]
        )
        copy.start()
        copies.append(copy)
    at = lax.broadcasted_iota(jnp.int32, rot.shape[1:], 0)
    bins = 1 + lax.broadcasted_iota(jnp.int32, rot.shape[1:], 1)
    times = at
    for step in range(doublings):
        times = jnp.where(at == BASE + step, BASE * 2**step, times)
    angle = (times * bins % length).astype(jnp.float32) * (2.0 * math.pi / length)
    rot[0] = jnp.cos(angle)
    rot[1] = jnp.sin(angle)
    cos_t[0:BASE] = rot[0, 0:BASE]
    sin_t[0:BASE] = rot[1, 0:BASE]
    done = BASE
    for step in range(doublings):
        ca, sa = rot[0, BASE + step : BASE + step + 1], rot[1, BASE + step : BASE + step + 1]
        c, s = cos_t[0:done], sin_t[0:done]
        cos_t[done : 2 * done] = c * ca - s * sa
        sin_t[done : 2 * done] = s * ca + c * sa
        done *= 2
    for h in range(2):
        table[:, h * BINS : h * BINS + half] = cos_t[:, h * half : (h + 1) * half].astype(jnp.bfloat16)
        table[:, h * BINS + half : (h + 1) * BINS] = (-sin_t[:, h * half : (h + 1) * half]).astype(jnp.bfloat16)
    turn = (1 + lax.broadcasted_iota(jnp.int32, (1, BINS), 1)) % 4
    for q in range(QUARTERS):
        if q % 2 == 0:
            copies[q].wait()
            copies[q + 1].wait()
        part = jnp.dot(block[q], table[...], preferred_element_type=jnp.float32)
        for h in range(2):
            re = part[:, h * BINS : h * BINS + half]
            im = part[:, h * BINS + half : (h + 1) * BINS]
            if q == 0:
                spec[2 * h], spec[2 * h + 1] = re, im
                continue
            power = turn[:, h * half : (h + 1) * half] * q % 4
            al = jnp.where(power == 0, 1.0, jnp.where(power == 2, -1.0, 0.0))
            be = jnp.where(power == 1, 1.0, jnp.where(power == 3, -1.0, 0.0))
            spec[2 * h] += re * al + im * be
            spec[2 * h + 1] += im * al - re * be
    squares = jnp.zeros((rows, LANES), jnp.float32)
    for tile in range(4):
        squares += spec[tile] * spec[tile]
    energy = jnp.sum(squares, axis=1, keepdims=True)
    scale[...] = jnp.broadcast_to(lax.rsqrt(energy / (2 * BINS) + EPSILON), scale.shape)
    for s in range(seg_cols):
        factor = scale[pl.ds(s, chans, stride=seg_cols), :]
        for r in range(2):
            for out, h in ((mine_out, freq), (other_out, 1 - freq)):
                value = spec[2 * h + r, pl.ds(s, chans, stride=seg_cols), :]
                out[2 * s + r] = (value * factor).astype(jnp.bfloat16)


def whitened_half(samples):
    chan_rows, seg_cols, length = samples.shape
    rows = chan_rows * seg_cols // 2
    quarter = length // QUARTERS
    doublings = int(math.log2(quarter // BASE))
    out = jax.ShapeDtypeStruct((2 * seg_cols, chan_rows // 2, BINS // 2), jnp.bfloat16)
    return pl.pallas_call(
        functools.partial(dft_kernel, length, doublings),
        in_specs=[HBM],
        out_specs=[VMEM, VMEM],
        out_shape=[out, out],
        scratch_shapes=[
            pltpu.VMEM((QUARTERS, rows, quarter), jnp.bfloat16),
            pltpu.VMEM((2, -(-(BASE + doublings) // 8) * 8, BINS), jnp.float32),
            pltpu.VMEM((quarter, BINS), jnp.float32),
            pltpu.VMEM((quarter, BINS), jnp.float32),
            pltpu.VMEM((quarter, 2 * BINS), jnp.bfloat16),
            pltpu.VMEM((2 * BINS // LANES, rows, LANES), jnp.float32),
            pltpu.VMEM((rows, LANES), jnp.float32),
            pltpu.SemaphoreType.DMA((QUARTERS,)),
        ],
        compiler_params=pltpu.CompilerParams(vmem_limit_bytes=48 << 20),
        cost_estimate=pl.CostEstimate(flops=4 * rows * length * BINS, bytes_accessed=2 * rows * length, transcendentals=0),
        name="dft_whiten",
    )(samples.reshape(chan_rows * seg_cols, length))


def cross_kernel(load, last, *refs):
    inverse, before = (refs[0], refs[1]) if last else (None, None)
    out, rows_re, rows_im, rows_sum, rows_dif, pairs = refs[-6:]
    segs = rows_re.shape[0]
    step = pl.program_id(0)

    @pl.when(step == 0)
    def _():
        load(refs[2 if last else 0 : -6], rows_re, rows_im)
        for s in range(segs):
            re, im = rows_re[s], rows_im[s]
            rows_sum[s] = re + im
            rows_dif[s] = re - im

    blocks = OFFSETS // 8

    def channel(n, carry):
        i = step * STEP + n
        k1 = [None] * blocks
        k2 = [None] * blocks
        k3 = [None] * blocks
        for s in range(segs):
            a_re = rows_re[s, pl.ds(i, 8, stride=0), :]
            a_sum = rows_sum[s, pl.ds(i, 8, stride=0), :]
            a_dif = rows_dif[s, pl.ds(i, 8, stride=0), :]
            for m in range(blocks):
                at = pl.ds(i + 8 * m, 8)
                t1 = a_re * rows_sum[s, at, :]
                t2 = a_dif * rows_im[s, at, :]
                t3 = a_sum * rows_re[s, at, :]
                k1[m] = t1 if s == 0 else k1[m] + t1
                k2[m] = t2 if s == 0 else k2[m] + t2
                k3[m] = t3 if s == 0 else k3[m] + t3
        for m in range(blocks):
            at = pl.ds(8 * m, 8)
            re, im = k1[m] - k2[m], k1[m] - k3[m]
            if not last:
                out[0, n, at, :] = re
                out[1, n, at, :] = im
                continue
            inv = inverse[n, at, :]
            pairs[pl.ds(16 * m, 8, stride=2), :] = (re + before[0, n, at, :]) * inv
            pairs[pl.ds(16 * m + 1, 8, stride=2), :] = (im + before[1, n, at, :]) * inv
        if last:
            out[n] = pairs[...].astype(jnp.bfloat16)
        return carry

    lax.fori_loop(0, STEP, channel, 0)


def cross_sums(load, arrays, owned, segs, width, finish=()):
    scratch = pltpu.VMEM((segs, width, LANES), jnp.float32)
    bins = arrays[0].shape[-1]
    result = (
        jax.ShapeDtypeStruct((owned, 2 * OFFSETS, bins), jnp.bfloat16)
        if finish
        else jax.ShapeDtypeStruct((2, owned, OFFSETS, bins), jnp.float32)
    )
    whole = lambda a: pl.BlockSpec(a.shape, lambda n: (0,) * a.ndim, pipeline_mode=pl.Buffered(1))
    sums = pl.BlockSpec((2, STEP, OFFSETS, bins), lambda n: (0, n, 0, 0))
    return pl.pallas_call(
        functools.partial(cross_kernel, load, bool(finish)),
        grid=(owned // STEP,),
        in_specs=([pl.BlockSpec((STEP, OFFSETS, bins), lambda n: (n, 0, 0)), sums] if finish else []) + [whole(a) for a in arrays],
        out_specs=pl.BlockSpec((STEP, 2 * OFFSETS, bins), lambda n: (n, 0, 0)) if finish else sums,
        out_shape=result,
        scratch_shapes=[scratch] * 4 + [pltpu.VMEM((2 * OFFSETS, LANES), jnp.float32)],
        compiler_params=pltpu.CompilerParams(vmem_limit_bytes=32 << 20),
        cost_estimate=pl.CostEstimate(flops=8 * owned * OFFSETS * segs * bins, bytes_accessed=owned * OFFSETS * bins * 4, transcendentals=0),
        name="cross_last" if finish else "cross_first",
    )(*finish, *arrays)


def inverse_pairs(live, first_row, owned):
    width = owned + OFFSETS
    padded = jnp.concatenate([live, jnp.zeros((OFFSETS, live.shape[1]), live.dtype)], axis=0)
    rows = lax.dynamic_slice_in_dim(padded, first_row, width, 0).astype(jnp.bfloat16)
    square = jnp.dot(rows, rows[:owned].T, preferred_element_type=jnp.float32)
    flat = square.T.reshape(owned * width)
    flat = jnp.concatenate([flat, jnp.zeros((owned,), flat.dtype)])
    band = flat.reshape(owned, width + 1)[:, :OFFSETS]
    return jnp.broadcast_to((1.0 / jnp.maximum(band, 1.0))[:, :, None], (owned, OFFSETS, LANES))


def split(value, segs, rows_re, rows_im, first_seg, first_row):
    count = value.shape[1]
    for s in range(segs):
        rows_re[first_seg + s, first_row : first_row + count, :] = value[2 * s].astype(jnp.float32)
        rows_im[first_seg + s, first_row : first_row + count, :] = value[2 * s + 1].astype(jnp.float32)


def clear_tail(rows_re, rows_im, width):
    for s in range(rows_re.shape[0]):
        rows_re[s, width:, :] = jnp.zeros((8, LANES), jnp.float32)
        rows_im[s, width:, :] = jnp.zeros((8, LANES), jnp.float32)


def load_own(segs, unit, refs, rows_re, rows_im):
    low, high, near, next_high = refs
    x = lax.axis_index("seg")
    clear_tail(rows_re, rows_im, 3 * unit)
    put = lambda value, row: split(value, segs, rows_re, rows_im, 0, row * unit)

    @pl.when(x == 0)
    def _():
        put(low[...], 0)
        put(high[...], 1)
        put(near[...], 2)

    @pl.when(x == 1)
    def _():
        put(high[...], 0)
        put(near[...], 1)
        put(next_high[...], 2)


def load_sent(segs, unit, refs, rows_re, rows_im):
    corner, side, swap = refs
    x = lax.axis_index("seg")
    clear_tail(rows_re, rows_im, 3 * unit)
    put = lambda value, row: split(value, segs, rows_re, rows_im, 0, row * unit)

    @pl.when(x == 0)
    def _():
        put(side[...], 0)
        put(swap[...], 1)
        put(corner[...], 2)

    @pl.when(x == 1)
    def _():
        put(swap[...], 0)
        put(corner[...], 1)
        put(side[...], 2)


def direct(low, high, live, unit):
    chan, z = lax.axis_size("chan"), lax.axis_index("chan")
    x = lax.axis_index("seg")
    at = lambda block, group: 2 * block + group
    send = lambda value, pairs: lax.ppermute(value, ("chan", "seg"), pairs)
    blocks, lower = range(chan), range(1, chan)
    across = [(at(b, g), at(b, 1 - g)) for b in blocks for g in range(2)]
    diagonal = [(at(b, g), at(b - 1, 1 - g)) for b in lower for g in range(2)]
    mixed = [(at(b, 1), at(b, 0)) for b in blocks] + [(at(b, 0), at(b - 1, 1)) for b in lower]
    below = [(at(b, g), at(b - 1, g)) for b in lower for g in range(2)]
    below_one = [(at(b, 1), at(b - 1, 1)) for b in lower]
    corner = send(low, diagonal)
    swap = send(high, across)
    near = send(low, below)
    next_high = send(high, below_one)
    side = send(jnp.where(x == 0, high, low), mixed)
    segs = low.shape[0] // 2
    inverse = inverse_pairs(live, (2 * z + x) * unit, unit)
    width = 3 * unit + 8
    near, inverse = lax.optimization_barrier((near, inverse))
    first = cross_sums(functools.partial(load_own, segs, unit), [low, high, near, next_high], unit, segs, width)
    out = cross_sums(functools.partial(load_sent, segs, unit), [corner, side, swap], unit, segs, width, (inverse, first))
    return out.reshape(unit, OFFSETS, 2, out.shape[-1])


def load_window(segs, width, group, refs, rows_re, rows_im):
    (window,) = refs
    split(window[group], segs, rows_re, rows_im, 0, 0)
    clear_tail(rows_re, rows_im, width)


def gathered(low, high, live, owned):
    groups, chan = lax.axis_size("seg"), lax.axis_size("chan")
    own = jnp.concatenate([low, high], axis=1)
    above = lax.ppermute(own[:, :OFFSETS], "chan", [(b, b - 1) for b in range(1, chan)])
    extended = jnp.concatenate([own, above], axis=1)
    width = owned + OFFSETS
    windows = jnp.stack([extended[:, t * owned : t * owned + width] for t in range(groups)])
    window = lax.all_to_all(windows, "seg", split_axis=0, concat_axis=0, tiled=True)
    segs = low.shape[0] // 2
    first_row = (lax.axis_index("chan") * groups + lax.axis_index("seg")) * owned
    inverse = inverse_pairs(live, first_row, owned)
    total = None
    for group in range(groups):
        finish = (inverse, total) if group == groups - 1 else ()
        load = functools.partial(load_window, segs, width, group)
        part = cross_sums(load, [window], owned, segs, width + 8, finish)
        total = part if finish or total is None else total + part
    return total.reshape(owned, OFFSETS, 2, total.shape[-1])


def shards(samples, live):
    mine, other = whitened_half(samples)
    theirs = lax.ppermute(other, "freq", [(0, 1), (1, 0)])
    freq = lax.axis_index("freq")
    rows, cols = samples.shape[:2]
    usable = lax.dynamic_slice(
        live, (lax.axis_index("chan") * rows, lax.axis_index("seg") * cols), (rows, cols)
    )
    usable = jnp.repeat(usable.T.astype(jnp.bfloat16), 2, axis=0)[:, :, None]
    low = jnp.where(freq == 0, mine, theirs) * usable[:, : rows // 2]
    high = jnp.where(freq == 0, theirs, mine) * usable[:, rows // 2 :]
    groups = lax.axis_size("seg")
    owned = samples.shape[0] // groups
    step = direct if groups == 2 and owned == OFFSETS // 2 else gathered
    return step(low, high, live, owned)


def solution(mesh):
    return jax.shard_map(
        shards,
        mesh=mesh,
        in_specs=(P(("cable", "chan"), "seg", None), P("cable", None)),
        out_specs=P(("cable", "chan", "seg"), None, None, "freq"),
        check_vma=False,
    )
```

time: 30.6 us -> 26.7 us (0.87)
  starting transfers between devices: 9.8 us -> 7.99 us
  waiting for transfers between devices: 8.96 us -> 7.62 us
  local copies, waits for them, and re-layouts: 1.82 us -> 0.6 us
    ppermute x4 -> x5, starting transfers between devices: 9.24 us -> 7.43 us  [direct(): send = lambda value, pairs: lax.ppermute(value, ('chan', 'seg'), pairs)]
    unnamed x7 -> x2, local copies, waits for them, and re-layouts: 1.64 us -> 0.01 us
    ppermute x4 -> x5, waiting for transfers between devices: 8.05 us -> 7.25 us  [direct(): send = lambda value, pairs: lax.ppermute(value, ('chan', 'seg'), pairs)]
    ppermute x1, waiting for transfers between devices: 0.91 us -> 0.37 us  [shards(): theirs = lax.ppermute(other, 'freq', [(0, 1), (1, 0)])]
    broadcast_in_dim x0 -> x2, local copies, waits for them, and re-layouts: none -> 0.33 us  [the longest x1 0.32 us: inverse_pairs(): jnp.broadcast_to((1.0 / jnp.maximum(band, 1.0))[:, :, None], (owned, OFFS...]
    pallas_call x2 -> x3, Pallas kernels: 9.34 us -> 9.61 us  [the longest x2 5.33 us: cross_sums(): pl.pallas_call(functools.partial(cross_kernel, load, bool(finish)), grid=...]
  transfers between devices with their start and end apart: 5 -> 6, of which waited for: 2 -> 2; matrix products, arithmetic and copies ran while one was open for 2% -> 4% of each run, Pallas kernels for 0% -> 8%
where the time goes in v2:
time: 26.7 us; the launch traced here: 26.5 us
  Pallas kernels  9.61 us (36%)
  starting transfers between devices  7.99 us (30%)
  waiting for transfers between devices  7.62 us (29%)
  local copies, waits for them, and re-layouts  0.6 us (2%)
  other arithmetic  0.37 us (1%)
    ppermute x5, starting transfers between devices, direct(): send = lambda value, pairs: lax.ppermute(value, ('chan', 'seg'), pairs)  7.43 us
    ppermute x5, waiting for transfers between devices, direct(): send = lambda value, pairs: lax.ppermute(value, ('chan', 'seg'), pairs)  7.25 us
    pallas_call x2, Pallas kernels, cross_sums(): pl.pallas_call(functools.partial(cross_kernel, load, bool(finish)), grid=...  5.33 us
    pallas_call x1, Pallas kernels, whitened_half(): pl.pallas_call(functools.partial(dft_kernel, length, doublings), in_specs...  4.28 us
    ppermute x1, starting transfers between devices, shards(): theirs = lax.ppermute(other, 'freq', [(0, 1), (1, 0)])  0.56 us
  transfers between devices with their start and end apart: 6, of which 2 were waited for; matrix products, arithmetic and copies ran while one was open for 4% of the time, Pallas kernels for 8%

profile of v2, /device:TPU:0, one launch (start us, length us, event | category | flops | bytes accessed | tf_op | source)
XLA Modules:
  0.0 26.5 jit_solution(12760093316017822437)
XLA Ops:
  0.0 0.0 copy-start
  0.0 4.3 %dft_whiten.1 = (bf16[16,32,128]{2,1,0:T(8,128)(2,1)S(1)}, bf16[16,32,128]{2,1,0:T(8,128)(2,1)S(1)}) custom-call(bf16[512,8192]{1,0:T(8,128)(2,1)} %bitcast.10), custom_call_target="tpu_custom_call" | custom-call | flops 2147483648 | bytes 4194304 | tf_op jit(solution)/shard_map/dft_whiten/pallas_call | solution.py:93
  4.3 0.6 %collective-permute-start = (bf16[16,32,128]{2,1,0:T(8,128)(2,1)S(1)}, bf16[16,32,128]{2,1,0:T(8,128)(2,1)S(1)}, u32[]{:S(2)}, u32[]{:S(2)}) collective-permute-start(bf16[16,32,128]{2,1,0:T(8,128)(2,1)S(1)} %get-tuple-element.10), channel_id=1, source_target_pairs={{0,1},{1,0},{2,3},{3,2},{4,5},{5,4},{6,7},{7,6},{8,9},{9,8},{10,11... | collective-permute-start | bytes 393224 | tf_op jit(solution)/shard_map/ppermute | solution.py:302
  4.9 0.0 copy-done
  4.9 0.1 fusion.1
  4.9 0.2 fusion.2
  5.1 0.1 reshape.14
  5.2 0.1 reshape.15
  5.3 0.1 fusion.4
  5.4 0.1 slice_bitcast_fusion.1
  5.5 0.4 %collective-permute-done = bf16[16,32,128]{2,1,0:T(8,128)(2,1)S(1)} collective-permute-done((bf16[16,32,128]{2,1,0:T(8,128)(2,1)S(1)}, bf16[16,32,128]{2,1,0:T(8,128)(2,1)S(1)}, u32[]{:S(2)}, u32[]{:S(2)}) %collective-permute-start) | collective-permute-done | bytes 131104 | tf_op jit(solution)/shard_map/ppermute | solution.py:302
  5.8 0.2 broadcast_select_fusion
  6.0 2.9 %collective-permute-start.5 = (bf16[16,32,128]{2,1,0:T(8,128)(2,1)S(1)}, bf16[16,32,128]{2,1,0:T(8,128)(2,1)S(1)}, u32[]{:S(2)}, u32[]{:S(2)}) collective-permute-start(bf16[16,32,128]{2,1,0:T(8,128)(2,1)S(1)} %get-tuple-element.14.refs_1_), channel_id=1, source_target_pairs={{0,2},{2,0},{4,6},{6,4},{8,10},{10,8},{12,14},{14,12},{1,3},{3,1},... | collective-permute-start | bytes 393224 | tf_op jit(solution)/shard_map/ppermute | solution.py:253
  8.9 0.7 %collective-permute-start.2 = (bf16[16,32,128]{2,1,0:T(8,128)(2,1)S(1)}, bf16[16,32,128]{2,1,0:T(8,128)(2,1)S(1)}, u32[]{:S(2)}, u32[]{:S(2)}) collective-permute-start(bf16[16,32,128]{2,1,0:T(8,128)(2,1)S(1)} %get-tuple-element.14.refs_1_), channel_id=1, source_target_pairs={{6,2},{10,6},{14,10},{7,3},{11,7},{15,11},{22,18},{26,22},{30,26},... | collective-permute-start | bytes 393224 | tf_op jit(solution)/shard_map/ppermute | solution.py:253
  9.6 1.3 %collective-permute-start.3 = (bf16[16,32,128]{2,1,0:T(8,128)(2,1)S(1)}, bf16[16,32,128]{2,1,0:T(8,128)(2,1)S(1)}, u32[]{:S(2)}, u32[]{:S(2)}) collective-permute-start(bf16[16,32,128]{2,1,0:T(8,128)(2,1)S(1)} %get-tuple-element.15.refs_0_), channel_id=1, source_target_pairs={{4,2},{6,0},{8,6},{10,4},{12,10},{14,8},{5,3},{7,1},{9,7},{11,5},{... | collective-permute-start | bytes 393224 | tf_op jit(solution)/shard_map/ppermute | solution.py:253
  10.9 1.3 %collective-permute-start.1 = (bf16[16,32,128]{2,1,0:T(8,128)(2,1)S(1)}, bf16[16,32,128]{2,1,0:T(8,128)(2,1)S(1)}, u32[]{:S(2)}, u32[]{:S(2)}) collective-permute-start(bf16[16,32,128]{2,1,0:T(8,128)(2,1)S(1)} %get-tuple-element.15.refs_0_), channel_id=1, source_target_pairs={{4,0},{6,2},{8,4},{10,6},{12,8},{14,10},{5,1},{7,3},{9,5},{11,7},{... | collective-permute-start | bytes 393224 | tf_op jit(solution)/shard_map/ppermute | solution.py:253
  12.2 1.3 %collective-permute-start.4 = (bf16[16,32,128]{2,1,0:T(8,128)(2,1)S(1)}, bf16[16,32,128]{2,1,0:T(8,128)(2,1)S(1)}, u32[]{:S(2)}, u32[]{:S(2)}) collective-permute-start(bf16[16,32,128]{2,1,0:T(8,128)(2,1)S(1)} %get-tuple-element.13), channel_id=1, source_target_pairs={{2,0},{6,4},{10,8},{14,12},{4,2},{8,6},{12,10},{3,1},{7,5},{11,9},... | collective-permute-start | bytes 393224 | tf_op jit(solution)/shard_map/ppermute | solution.py:253
  13.5 7.2 %collective-permute-done.1.refs_2_ = bf16[16,32,128]{2,1,0:T(8,128)(2,1)S(1)} collective-permute-done((bf16[16,32,128]{2,1,0:T(8,128)(2,1)S(1)}, bf16[16,32,128]{2,1,0:T(8,128)(2,1)S(1)}, u32[]{:S(2)}, u32[]{:S(2)}) %collective-permute-start.1) | collective-permute-done | bytes 131104 | tf_op jit(solution)/shard_map/ppermute | solution.py:253
  20.8 0.3 %broadcast_in_dim.5.refs_0_ = f32[32,64,128]{2,1,0:T(8,128)S(1)} broadcast(f32[32,64]{1,0:T(8,128)S(1)} %fusion), dimensions={0,1} | broadcast | bytes 1056768 | tf_op jit(solution)/shard_map/broadcast_in_dim | solution.py:195
  21.1 0.0 collective-permute-done.2.refs_3_
  21.1 2.0 %cross_first.1.refs_1_ = f32[2,32,64,128]{3,2,1,0:T(8,128)S(1)} custom-call(bf16[16,32,128]{2,1,0:T(8,128)(2,1)S(1)} %get-tuple-element.15.refs_0_, bf16[16,32,128]{2,1,0:T(8,128)(2,1)S(1)} %get-tuple-element.14.refs_1_, bf16[16,32,128]{2,1,0:T(8,128)(2,1)S(1)} %collective-permute-done.1.refs_2_, bf16[16,32,128]{2,1,0:T(8,128)(2,1)S(1)} %collective-permute-done.2.refs_3_), custom_call_target="tpu_custom_call" | custom-call | flops 16777216 | bytes 1048576 | tf_op jit(solution)/shard_map/cross_first/pallas_call | solution.py:174
  23.2 0.0 collective-permute-done.4.refs_3_
  23.2 0.0 collective-permute-done.5.refs_4_
  23.2 0.0 collective-permute-done.3.refs_2_
  23.2 3.3 %cross_last.1 = bf16[32,128,128]{2,1,0:T(8,128)(2,1)} custom-call(f32[32,64,128]{2,1,0:T(8,128)S(1)} %broadcast_in_dim.5.refs_0_, f32[2,32,64,128]{3,2,1,0:T(8,128)S(1)} %cross_first.1.refs_1_, bf16[16,32,128]{2,1,0:T(8,128)(2,1)S(1)} %collective-permute-done.3.refs_2_, bf16[16,32,128]{2,1,0:T(8,128)(2,1)S(1)} %collective-permute-done.4.refs_3_, ...), custom_call_target="tpu_custom_call" | custom-call | flops 16777216 | bytes 1048576 | tf_op jit(solution)/shard_map/cross_last/pallas_call | solution.py:174
  (3 shorter events, 0.0 us)
Async XLA Ops:
  0.0 4.9 %copy-start = (s32[256,16]{0,1:T(8,128)S(1)}, s32[256,16]{0,1:T(8,128)}, u32[]{:S(2)}) copy-start(s32[256,16]{0,1:T(8,128)} %param.3) | copy-start | bytes 49156
  4.3 1.5 %collective-permute-start = (bf16[16,32,128]{2,1,0:T(8,128)(2,1)S(1)}, bf16[16,32,128]{2,1,0:T(8,128)(2,1)S(1)}, u32[]{:S(2)}, u32[]{:S(2)}) collective-permute-start(bf16[16,32,128]{2,1,0:T(8,128)(2,1)S(1)} %get-tuple-element.10), channel_id=1, source_target_pairs={{0,1},{1,0},{2,3},{3,2},{4,5},{5,4},{6,7},{7,6},{8,9},{9,8},{10,11... | collective-permute-start | bytes 393224 | tf_op jit(solution)/shard_map/ppermute | solution.py:302
  6.0 17.1 %collective-permute-start.5 = (bf16[16,32,128]{2,1,0:T(8,128)(2,1)S(1)}, bf16[16,32,128]{2,1,0:T(8,128)(2,1)S(1)}, u32[]{:S(2)}, u32[]{:S(2)}) collective-permute-start(bf16[16,32,128]{2,1,0:T(8,128)(2,1)S(1)} %get-tuple-element.14.refs_1_), channel_id=1, source_target_pairs={{0,2},{2,0},{4,6},{6,4},{8,10},{10,8},{12,14},{14,12},{1,3},{3,1},... | collective-permute-start | bytes 393224 | tf_op jit(solution)/shard_map/ppermute | solution.py:253
  8.9 12.2 %collective-permute-start.2 = (bf16[16,32,128]{2,1,0:T(8,128)(2,1)S(1)}, bf16[16,32,128]{2,1,0:T(8,128)(2,1)S(1)}, u32[]{:S(2)}, u32[]{:S(2)}) collective-permute-start(bf16[16,32,128]{2,1,0:T(8,128)(2,1)S(1)} %get-tuple-element.14.refs_1_), channel_id=1, source_target_pairs={{6,2},{10,6},{14,10},{7,3},{11,7},{15,11},{22,18},{26,22},{30,26},... | collective-permute-start | bytes 393224 | tf_op jit(solution)/shard_map/ppermute | solution.py:253
  9.6 13.6 %collective-permute-start.3 = (bf16[16,32,128]{2,1,0:T(8,128)(2,1)S(1)}, bf16[16,32,128]{2,1,0:T(8,128)(2,1)S(1)}, u32[]{:S(2)}, u32[]{:S(2)}) collective-permute-start(bf16[16,32,128]{2,1,0:T(8,128)(2,1)S(1)} %get-tuple-element.15.refs_0_), channel_id=1, source_target_pairs={{4,2},{6,0},{8,6},{10,4},{12,10},{14,8},{5,3},{7,1},{9,7},{11,5},{... | collective-permute-start | bytes 393224 | tf_op jit(solution)/shard_map/ppermute | solution.py:253
  10.9 9.9 %collective-permute-start.1 = (bf16[16,32,128]{2,1,0:T(8,128)(2,1)S(1)}, bf16[16,32,128]{2,1,0:T(8,128)(2,1)S(1)}, u32[]{:S(2)}, u32[]{:S(2)}) collective-permute-start(bf16[16,32,128]{2,1,0:T(8,128)(2,1)S(1)} %get-tuple-element.15.refs_0_), channel_id=1, source_target_pairs={{4,0},{6,2},{8,4},{10,6},{12,8},{14,10},{5,1},{7,3},{9,5},{11,7},{... | collective-permute-start | bytes 393224 | tf_op jit(solution)/shard_map/ppermute | solution.py:253
  12.2 11.0 %collective-permute-start.4 = (bf16[16,32,128]{2,1,0:T(8,128)(2,1)S(1)}, bf16[16,32,128]{2,1,0:T(8,128)(2,1)S(1)}, u32[]{:S(2)}, u32[]{:S(2)}) collective-permute-start(bf16[16,32,128]{2,1,0:T(8,128)(2,1)S(1)} %get-tuple-element.13), channel_id=1, source_target_pairs={{2,0},{6,4},{10,8},{14,12},{4,2},{8,6},{12,10},{3,1},{7,5},{11,9},... | collective-permute-start | bytes 393224 | tf_op jit(solution)/shard_map/ppermute | solution.py:253
